TPU v7x, 256 devices: a whole 4x4x8 slice. The times are simulated.
256 devices in a mesh: dp: 8 (over x, z_lo), seq: 32 (over y, z_hi, core).
Axes of the slice: x: 4, y: 4, z: 8 (z_hi: 4, z_lo: 2; z = z_hi * 2 + z_lo), core: 2. Of those that a mesh axis runs over, the one named last changes fastest.
Arguments:
- queries: bfloat16 [8, 32, 512, 1024], P('dp', 'seq'), may hold values from -16 to 16
- keys: bfloat16 [8, 32, 512, 1024], P('dp', 'seq'), may hold values from -12 to 12
- values: bfloat16 [8, 32, 512, 1024], P('dp', 'seq'), may hold values from -24 to 24
- out_proj: bfloat16 [1024, 2048], P(('dp', 'seq')), may hold values from -0.1875 to 0.1875
- out_grad: bfloat16 [8, 32, 512, 2048], P('dp', 'seq'), may hold values from -48 to 48
- block_pattern: int32 [4, 4], replicated, may hold values from 0 to 3, as said below
- col_offset: int32 [4], replicated, may hold values from 0 to 511
Outputs:
- layer_out: bfloat16 [8, 32, 512, 2048], P('dp', 'seq')
- q_grad: bfloat16 [8, 32, 512, 1024], P('dp', 'seq')
- k_grad: bfloat16 [8, 32, 512, 1024], P('dp', 'seq')
- v_grad: bfloat16 [8, 32, 512, 1024], P('dp', 'seq')
- w_grad: float32 [1024, 2048], P(('dp', 'seq'))
Inputs may be any that keep to these rules, and one draw needn't show every extreme that they name: `block_pattern`: for each row head, the entries name each of the 4 blocks of a grid row once, and entry j is never j.
All inputs are finite; a program needn't handle non-finite values.
Results may differ from a plain program's by a relative error of at most 0.006.
Values may be sent and summed in bfloat16 or wider, within the bound.
No kernel may reach another device: no remote copies, remote signals or barrier semaphores. Data moves between devices by JAX's collectives and lax.ppermute only.
A program may use at most 128 MiB of HBM per device.

v0:
```python
import jax
import jax.numpy as jnp
from jax import lax
from jax.sharding import PartitionSpec as P

HD = 128
HR = 4
HC = 4
BLK = 128
NB = 4


def block_selector(block_pattern):
    numbers = jnp.arange(NB, dtype=jnp.int32)
    return (block_pattern.T[:, :, None] == numbers[None, None, :]).astype(jnp.bfloat16)


def roll_columns(tensor, col_offset, direction):
    moved_heads = [
        jnp.roll(tensor[:, :, head_idx], direction * col_offset[head_idx], axis=1)
        for head_idx in range(HC)
    ]
    return jnp.stack(moved_heads, axis=2)


def column_forward(parts):
    query_cols, key_cols, value_cols = parts
    score_scale = HD ** (-0.5)
    scores = (
        jnp.einsum("rchd,schd->rchs", query_cols, key_cols, preferred_element_type=jnp.float32)
        * score_scale
    )
    col_probs = jax.nn.softmax(scores, axis=-1)
    col_out = jnp.einsum(
        "rchs,schd->rchd",
        col_probs.astype(jnp.bfloat16),
        value_cols,
        preferred_element_type=jnp.float32,
    ).astype(jnp.bfloat16)
    return (col_out, col_probs, query_cols, key_cols, value_cols)


def column_backward(query_cols, key_cols, value_cols, col_probs, grad_cols):
    score_scale = HD ** (-0.5)
    prob_half = col_probs.astype(jnp.bfloat16)
    value_grad = jnp.einsum(
        "rchs,rchd->schd", prob_half, grad_cols, preferred_element_type=jnp.float32
    ).astype(jnp.bfloat16)
    prob_grad = jnp.einsum(
        "rchd,schd->rchs", grad_cols, value_cols, preferred_element_type=jnp.float32
    )
    delta_sum = jnp.sum(col_probs * prob_grad, axis=-1, keepdims=True)
    score_grad = (col_probs * (prob_grad - delta_sum)).astype(jnp.bfloat16)
    query_grad = (
        jnp.einsum("rchs,schd->rchd", score_grad, key_cols, preferred_element_type=jnp.float32)
        * score_scale
    ).astype(jnp.bfloat16)
    key_grad = (
        jnp.einsum("rchs,rchd->schd", score_grad, query_cols, preferred_element_type=jnp.float32)
        * score_scale
    ).astype(jnp.bfloat16)
    return (query_grad, key_grad, value_grad)


def row_forward(query_rows, key_rows, value_rows, selector):
    score_scale = HD ** (-0.5)
    key_other = jnp.einsum(
        "jhm,rmbhd->rjbhd", selector, key_rows, preferred_element_type=jnp.float32
    ).astype(jnp.bfloat16)
    value_other = jnp.einsum(
        "jhm,rmbhd->rjbhd", selector, value_rows, preferred_element_type=jnp.float32
    ).astype(jnp.bfloat16)
    key_joined = jnp.concatenate([key_other, key_rows], axis=2)
    value_joined = jnp.concatenate([value_other, value_rows], axis=2)
    scores = (
        jnp.einsum("rjqhd,rjkhd->rjhqk", query_rows, key_joined, preferred_element_type=jnp.float32)
        * score_scale
    )
    row_probs = jax.nn.softmax(scores, axis=-1)
    row_out = jnp.einsum(
        "rjhqk,rjkhd->rjqhd",
        row_probs.astype(jnp.bfloat16),
        value_joined,
        preferred_element_type=jnp.float32,
    ).astype(jnp.bfloat16)
    return (row_out, row_probs, key_joined, value_joined)


def fold_back(term_sums, selector):
    own_part = term_sums[:, :, BLK:]
    moved_part = jnp.einsum(
        "jhm,rjbhd->rmbhd",
        selector.astype(jnp.float32),
        term_sums[:, :, :BLK],
        precision=lax.Precision.HIGHEST,
    )
    return (own_part + moved_part).astype(jnp.bfloat16)


def row_backward(query_rows, key_joined, value_joined, row_probs, grad_rows, selector):
    score_scale = HD ** (-0.5)
    prob_half = row_probs.astype(jnp.bfloat16)
    value_terms = jnp.einsum(
        "rjhqk,rjqhd->rjkhd", prob_half, grad_rows, preferred_element_type=jnp.float32
    )
    prob_grad = jnp.einsum(
        "rjqhd,rjkhd->rjhqk", grad_rows, value_joined, preferred_element_type=jnp.float32
    )
    delta_sum = jnp.sum(row_probs * prob_grad, axis=-1, keepdims=True)
    score_grad = (row_probs * (prob_grad - delta_sum)).astype(jnp.bfloat16)
    query_grad = (
        jnp.einsum("rjhqk,rjkhd->rjqhd", score_grad, key_joined, preferred_element_type=jnp.float32)
        * score_scale
    ).astype(jnp.bfloat16)
    key_terms = (
        jnp.einsum("rjhqk,rjqhd->rjkhd", score_grad, query_rows, preferred_element_type=jnp.float32)
        * score_scale
    )
    return (query_grad, fold_back(key_terms, selector), fold_back(value_terms, selector))


def shards(queries, keys, values, out_proj, out_grad, block_pattern, col_offset):
    row_count = queries.shape[1]
    col_count = queries.shape[2]
    feat_width = queries.shape[3]
    model_width = out_grad.shape[3]
    head_count = feat_width // HD
    token_count = row_count * col_count
    query_heads = queries.reshape(row_count, col_count, head_count, HD)
    key_heads = keys.reshape(row_count, col_count, head_count, HD)
    value_heads = values.reshape(row_count, col_count, head_count, HD)
    selector = block_selector(block_pattern)
    grad_flat = out_grad.reshape(token_count, model_width)
    attn_grad = lax.dot_general(
        grad_flat,
        lax.all_gather(out_proj, ("dp", "seq"), axis=0, tiled=True),
        (((1,), (1,)), ((), ())),
        preferred_element_type=jnp.float32,
    ).astype(jnp.bfloat16)
    grad_heads = attn_grad.reshape(row_count, col_count, head_count, HD)
    key_shift = roll_columns(key_heads[:, :, HR:], col_offset, 1)
    value_shift = roll_columns(value_heads[:, :, HR:], col_offset, 1)
    row_shape = (row_count, NB, BLK, HR, HD)
    query_rows = query_heads[:, :, :HR].reshape(row_shape)
    col_out, col_probs, query_cols, key_cols, value_cols = column_forward(
        (
            lax.all_to_all(query_heads[:, :, HR:], "seq", split_axis=1, concat_axis=0, tiled=True),
            lax.all_to_all(key_shift, "seq", split_axis=1, concat_axis=0, tiled=True),
            lax.all_to_all(value_shift, "seq", split_axis=1, concat_axis=0, tiled=True),
        )
    )
    row_out, row_probs, key_joined, value_joined = row_forward(
        query_rows,
        key_heads[:, :, :HR].reshape(row_shape),
        value_heads[:, :, :HR].reshape(row_shape),
        selector,
    )
    col_back = lax.all_to_all(col_out, "seq", split_axis=0, concat_axis=1, tiled=True)
    grad_cols = lax.all_to_all(
        grad_heads[:, :, HR:], "seq", split_axis=1, concat_axis=0, tiled=True
    )
    col_query_grad, col_key_grad, col_value_grad = column_backward(
        query_cols, key_cols, value_cols, col_probs, grad_cols
    )
    query_back, key_back, value_back = (
        lax.all_to_all(col_query_grad, "seq", split_axis=0, concat_axis=1, tiled=True),
        lax.all_to_all(col_key_grad, "seq", split_axis=0, concat_axis=1, tiled=True),
        lax.all_to_all(col_value_grad, "seq", split_axis=0, concat_axis=1, tiled=True),
    )
    attention = jnp.concatenate(
        [row_out.reshape(row_count, col_count, HR, HD), col_back], axis=2
    ).reshape(token_count, feat_width)
    attn_part = attention
    layer_sum = jnp.dot(
        attn_part,
        lax.all_gather(out_proj, ("dp", "seq"), axis=0, tiled=True),
        preferred_element_type=jnp.float32,
    )
    data_count = lax.axis_size("dp")
    seq_count = lax.axis_size("seq")
    attn_part = attention
    summed_grad = lax.psum_scatter(
        lax.dot_general(
            attn_part, grad_flat, (((0,), (0,)), ((), ())), preferred_element_type=jnp.float32
        ),
        ("dp", "seq"),
        scatter_dimension=0,
        tiled=True,
    )
    w_grad = summed_grad * (data_count * seq_count * token_count) ** (-0.5)
    key_back = roll_columns(key_back, col_offset, -1)
    value_back = roll_columns(value_back, col_offset, -1)
    row_query_grad, row_key_grad, row_value_grad = row_backward(
        query_rows,
        key_joined,
        value_joined,
        row_probs,
        grad_heads[:, :, :HR].reshape(row_shape),
        selector,
    )

    def assemble(row_part, col_part):
        return jnp.concatenate(
            [row_part.reshape(row_count, col_count, HR, HD), col_part], axis=2
        ).reshape(1, row_count, col_count, feat_width)

    layer_out = layer_sum.astype(jnp.bfloat16).reshape(1, row_count, col_count, model_width)
    return (
        layer_out,
        assemble(row_query_grad, query_back),
        assemble(row_key_grad, key_back),
        assemble(row_value_grad, value_back),
        w_grad,
    )


def solution(mesh):
    in_specs = (
        P("dp", "seq", None, None),
        P("dp", "seq", None, None),
        P("dp", "seq", None, None),
        P(("dp", "seq"), None),
        P("dp", "seq", None, None),
        P(),
        P(),
    )
    out_specs = (
        P("dp", "seq", None, None),
        P("dp", "seq", None, None),
        P("dp", "seq", None, None),
        P("dp", "seq", None, None),
        P(("dp", "seq"), None),
    )
    return jax.shard_map(shards, mesh=mesh, in_specs=in_specs, out_specs=out_specs, check_vma=False)
```

profile of v0, /device:TPU:1, one launch (start us, length us, event | category | flops | bytes accessed | tf_op | source)
XLA Modules:
  0.0 978.9 jit_solution(12304957022160518582)
XLA Ops:
  9.9 2.1 copy.246
  12.0 12.8 %all-to-all-start.2 = ((bf16[1,512,4,128]{3,2,0,1:T(4,128)(2,1)}), bf16[1,512,4,128]{3,2,0,1:T(4,128)(2,1)}, u32[]{:S(2)}, u32[]{:S(2)}) async-start(bf16[1,512,4,128]{3,2,0,1:T(4,128)(2,1)} %copy.246), calls=%async_computation.2 | async-start | bytes 1048576 | tf_op jit(solution)/shard_map/all_to_all | solution.py:147
  36.3 2.3 copy.215
  53.0 2.1 fusion.90
  58.5 9.8 %all-to-all-start.1 = ((bf16[1,512,4,128]{3,2,0,1:T(4,128)(2,1)}), bf16[1,512,4,128]{3,2,0,1:T(4,128)(2,1)}, u32[]{:S(2)}, u32[]{:S(2)}) async-start(bf16[1,512,4,128]{3,2,0,1:T(4,128)(2,1)} %copy.244), calls=%async_computation.1 | async-start | bytes 1048576 | tf_op jit(solution)/shard_map/all_to_all | solution.py:148
  70.5 15.7 %all-to-all-done.1 = bf16[1,512,4,128]{3,2,0,1:T(4,128)(2,1)} async-done(((bf16[1,512,4,128]{3,2,0,1:T(4,128)(2,1)}), bf16[1,512,4,128]{3,2,0,1:T(4,128)(2,1)}, u32[]{:S(2)}, u32[]{:S(2)}) %all-to-all-start.1) | async-done | bytes 524320 | tf_op jit(solution)/shard_map/all_to_all | solution.py:148
  86.2 6.3 all-to-all-start
  102.9 2.7 maximum_bitcast_fusion
  110.7 2.8 fusion.122
  117.5 10.0 %all-to-all-start.3 = ((bf16[32,16,4,128]{3,2,1,0:T(4,128)(2,1)}), bf16[32,16,4,128]{3,2,1,0:T(4,128)(2,1)}, u32[]{:S(2)}, u32[]{:S(2)}) async-start(bf16[32,16,4,128]{3,2,1,0:T(4,128)(2,1)} %copy.252), calls=%async_computation.3 | async-start | bytes 1048576 | tf_op jit(solution)/shard_map/all_to_all | solution.py:158
  132.8 12.5 %all-to-all-done.3 = bf16[32,16,4,128]{3,2,1,0:T(4,128)(2,1)} async-done(((bf16[32,16,4,128]{3,2,1,0:T(4,128)(2,1)}), bf16[32,16,4,128]{3,2,1,0:T(4,128)(2,1)}, u32[]{:S(2)}, u32[]{:S(2)}) %all-to-all-start.3) | async-done | bytes 524320 | tf_op jit(solution)/shard_map/all_to_all | solution.py:158
  146.5 2.1 pad_maximum_fusion
  148.6 2.3 copy.254
  150.9 6.8 fusion.3
  161.1 270.5 %all-reduce.3.cloned.1.call-done = f32[1024,2048]{1,0:T(8,128)} async-done(((f32[1024,2048]{1,0:T(8,128)}), f32[1024,2048]{1,0:T(8,128)}) %all-reduce.3.cloned.1.call-update) | async-done | bytes 8388624
  433.1 413.8 %all-gather.3.cloned.1.call-done = bf16[256,4,2048]{2,1,0:T(4,128)(2,1)} async-done(((bf16[1,4,2048]{2,1,0:T(4,128)(2,1)}), bf16[256,4,2048]{2,1,0:T(4,128)(2,1)}) %all-gather.3.cloned.1.call-update) | async-done | bytes 4194320 | tf_op jit(solution)/shard_map/all_gather | solution.py:176
  846.9 6.9 reshape.197
  853.8 4.5 fusion.16
  860.8 8.3 all-to-all-start.4
  878.3 8.8 all-to-all-done.4
  892.5 5.3 all-to-all-start.5
  897.8 2.3 slice_bitcast_fusion
  900.1 2.5 copy.282
  902.6 3.3 fusion.113
  905.9 2.6 copy.283
  908.5 2.5 fusion.32
  912.3 3.5 all-to-all-done.5
  915.8 6.5 all-to-all-start.6
  923.6 6.0 fusion.2
  931.0 9.3 all-to-all-done.6
  940.4 4.8 all-to-all-start.7
  954.3 8.9 all-to-all-done.7
  (153 shorter events, 93.0 us)
Async XLA Ops:
  7.2 143.7 %copy-start = (bf16[1,1,512,2048]{3,2,1,0:T(8,128)(2,1)S(1)}, bf16[1,1,512,2048]{3,2,1,0:T(8,128)(2,1)}, u32[]{:S(2)}) copy-start(bf16[1,1,512,2048]{3,2,1,0:T(8,128)(2,1)} %param.13) | copy-start | bytes 6291460
  8.8 16.0 %copy-start.28 = (s32[4]{0:T(128)S(1)}, s32[4]{0:T(128)}, u32[]{:S(2)}) copy-start(s32[4]{0:T(128)} %param.15) | copy-start | bytes 52
  12.0 46.5 %all-to-all-start.2 = ((bf16[1,512,4,128]{3,2,0,1:T(4,128)(2,1)}), bf16[1,512,4,128]{3,2,0,1:T(4,128)(2,1)}, u32[]{:S(2)}, u32[]{:S(2)}) async-start(bf16[1,512,4,128]{3,2,0,1:T(4,128)(2,1)} %copy.246), calls=%async_computation.2 | async-start | bytes 1048576 | tf_op jit(solution)/shard_map/all_to_all | solution.py:147
  53.0 15.3 %copy-start.24 = (bf16[1,512,1,128]{3,1,2,0:T(8,128)(2,1)S(1)}, bf16[1,512,1,128]{3,1,2,0:T(8,128)(2,1)}, u32[]{:S(2)}) copy-start(bf16[1,512,1,128]{3,1,2,0:T(8,128)(2,1)} %get-tuple-element.52) | copy-start | bytes 393220
  55.1 13.2 %copy-start.25 = (bf16[1,512,1,128]{3,1,2,0:T(8,128)(2,1)S(1)}, bf16[1,512,1,128]{3,1,2,0:T(8,128)(2,1)}, u32[]{:S(2)}) copy-start(bf16[1,512,1,128]{3,1,2,0:T(8,128)(2,1)} %get-tuple-element.54) | copy-start | bytes 393220
  57.2 11.1 %copy-start.26 = (bf16[1,512,1,128]{3,1,2,0:T(8,128)(2,1)S(1)}, bf16[1,512,1,128]{3,1,2,0:T(8,128)(2,1)}, u32[]{:S(2)}) copy-start(bf16[1,512,1,128]{3,1,2,0:T(8,128)(2,1)} %get-tuple-element.56) | copy-start | bytes 393220
  58.5 27.8 %all-to-all-start.1 = ((bf16[1,512,4,128]{3,2,0,1:T(4,128)(2,1)}), bf16[1,512,4,128]{3,2,0,1:T(4,128)(2,1)}, u32[]{:S(2)}, u32[]{:S(2)}) async-start(bf16[1,512,4,128]{3,2,0,1:T(4,128)(2,1)} %copy.244), calls=%async_computation.1 | async-start | bytes 1048576 | tf_op jit(solution)/shard_map/all_to_all | solution.py:148
  86.2 27.3 %all-to-all-start = ((bf16[1,512,4,128]{3,2,0,1:T(4,128)(2,1)}), bf16[1,512,4,128]{3,2,0,1:T(4,128)(2,1)}, u32[]{:S(2)}, u32[]{:S(2)}) async-start(bf16[1,512,4,128]{3,2,0,1:T(4,128)(2,1)} %copy.238), calls=%async_computation | async-start | bytes 1048576 | tf_op jit(solution)/shard_map/all_to_all | solution.py:149
  96.6 5.8 copy-start.27
  102.3 3.9 copy-start.13
  114.6 1.8 copy-start.21
  117.5 27.9 %all-to-all-start.3 = ((bf16[32,16,4,128]{3,2,1,0:T(4,128)(2,1)}), bf16[32,16,4,128]{3,2,1,0:T(4,128)(2,1)}, u32[]{:S(2)}, u32[]{:S(2)}) async-start(bf16[32,16,4,128]{3,2,1,0:T(4,128)(2,1)} %copy.252), calls=%async_computation.3 | async-start | bytes 1048576 | tf_op jit(solution)/shard_map/all_to_all | solution.py:158
  127.5 304.1 %all-reduce.3.cloned.1.call-start = ((), (), s32[]{:S(2)}) async-start(), calls=%async_computation.9 | async-start | bytes 16777216
  129.0 1.7 copy-start.16
  157.8 689.1 %all-gather.3.cloned.1.call-start = ((), (), s32[]{:S(2)}) async-start(), calls=%async_computation.8 | async-start | bytes 4210688 | tf_op jit(solution)/shard_map/all_gather | solution.py:176
  859.7 11.0 %copy-start.3 = (f32[4,4,128,256]{2,3,1,0:T(8,128)S(1)}, f32[4,4,128,256]{2,3,1,0:T(8,128)}, u32[]{:S(2)}) copy-start(f32[4,4,128,256]{2,3,1,0:T(8,128)} %copy-done.2) | copy-start | bytes 6291460
  860.8 26.3 %all-to-all-start.4 = ((bf16[1,512,4,128]{3,2,0,1:T(4,128)(2,1)}), bf16[1,512,4,128]{3,2,0,1:T(4,128)(2,1)}, u32[]{:S(2)}, u32[]{:S(2)}) async-start(bf16[1,512,4,128]{3,2,0,1:T(4,128)(2,1)} %slice.155), calls=%async_computation.4 | async-start | bytes 1048576 | tf_op jit(solution)/shard_map/all_to_all | solution.py:159
  870.7 1.6 copy-start.4
  876.5 11.8 %copy-start.18 = (f32[32,16,4,32]{0,3,2,1:T(8,128)S(1)}, f32[32,16,4,32]{0,3,2,1:T(8,128)}, u32[]{:S(2)}) copy-start(f32[32,16,4,32]{0,3,2,1:T(8,128)} %get-tuple-element.44) | copy-start | bytes 786436
  888.2 1.8 copy-start.22
  888.3 1.8 copy-start.19
  892.5 23.3 %all-to-all-start.5 = ((bf16[32,16,4,128]{3,2,1,0:T(4,128)(2,1)}), bf16[32,16,4,128]{3,2,1,0:T(4,128)(2,1)}, u32[]{:S(2)}, u32[]{:S(2)}) async-start(bf16[32,16,4,128]{3,2,1,0:T(4,128)(2,1)} %copy.269), calls=%async_computation.5 | async-start | bytes 1048576 | tf_op jit(solution)/shard_map/all_to_all | solution.py:166
  905.9 5.1 copy-start.7
  915.8 24.5 %all-to-all-start.6 = ((bf16[32,16,4,128]{3,2,1,0:T(4,128)(2,1)}), bf16[32,16,4,128]{3,2,1,0:T(4,128)(2,1)S(1)}, u32[]{:S(2)}, u32[]{:S(2)}) async-start(bf16[32,16,4,128]{3,2,1,0:T(4,128)(2,1)} %copy.277), calls=%async_computation.6 | async-start | bytes 1048576 | tf_op jit(solution)/shard_map/all_to_all | solution.py:167
  923.6 6.0 copy-start.20
  923.6 6.0 copy-start.23
  929.9 15.2 %copy-start.10 = (bf16[1,4,128,4,128]{4,2,1,3,0:T(8,128)(2,1)S(1)}, bf16[1,4,128,4,128]{4,2,1,3,0:T(8,128)(2,1)}, u32[]{:S(2)}) copy-start(bf16[1,4,128,4,128]{4,2,1,3,0:T(8,128)(2,1)} %copy.275) | copy-start | bytes 1572868
  929.9 16.1 %copy-start.9 = (bf16[1,4,128,4,128]{2,4,3,1,0:T(8,128)(2,1)S(1)}, bf16[1,4,128,4,128]{2,4,3,1,0:T(8,128)(2,1)}, u32[]{:S(2)}) copy-start(bf16[1,4,128,4,128]{2,4,3,1,0:T(8,128)(2,1)} %fusion.32) | copy-start | bytes 1572868
  940.4 6.0 copy-start.11
  940.4 22.9 %all-to-all-start.7 = ((bf16[32,16,4,128]{3,2,1,0:T(4,128)(2,1)}), bf16[32,16,4,128]{3,2,1,0:T(4,128)(2,1)}, u32[]{:S(2)}, u32[]{:S(2)}) async-start(bf16[32,16,4,128]{3,2,1,0:T(4,128)(2,1)} %copy.286), calls=%async_computation.7 | async-start | bytes 1048576 | tf_op jit(solution)/shard_map/all_to_all | solution.py:168
  946.0 2.2 copy-start.14
  967.9 4.0 copy-start.1
  (7 other events, 8.5 us)
Sparse Core Ops, SparseCore 0:
  157.9 273.6 all-reduce.2
  433.6 413.1 all-gather.2
where the time goes:
time: 986 us; the launch traced here: 979 us
  waiting for transfers between devices  744 us (75%)
  local copies, waits for them, and re-layouts  82 us (8%)
  starting transfers between devices  64 us (6%)
  matrix products  36.2 us (4%)
  other arithmetic  27.8 us (3%)
  between operations  25.1 us (3%)
    all_gather x1, waiting for transfers between devices, shards(): lax.all_gather(out_proj, ('dp', 'seq'), axis=0, tiled=True)  414 us
    unnamed x3, waiting for transfers between devices  271 us
    unnamed x69, local copies, waits for them, and re-layouts  22.3 us
  transfers between devices with their start and end apart: 10, of which 8 were waited for; matrix products, arithmetic and copies ran while one was open for 10% of the time, Pallas kernels for 0%

commit v1 on v0

--- a/solution.py
+++ b/solution.py
@@ -173,7 +173,12 @@
     attn_part = attention
     layer_sum = jnp.dot(
         attn_part,
-        lax.all_gather(out_proj, ("dp", "seq"), axis=0, tiled=True),
+        jnp.concatenate(
+            lax.all_to_all(
+                jnp.stack([out_proj] * lax.axis_size(("dp", "seq"))), ("dp", "seq"), 0, 0
+            ),
+            axis=0,
+        ),
         preferred_element_type=jnp.float32,
     )
     data_count = lax.axis_size("dp")

time: 986 us -> 960 us (0.974)
  waiting for transfers between devices: 744 us -> 686 us
  local copies, waits for them, and re-layouts: 82 us -> 97.1 us
  starting transfers between devices: 64 us -> 75.5 us
    all_gather x1, waiting for transfers between devices: 414 us -> 299 us  [shards(): lax.all_gather(out_proj, ('dp', 'seq'), axis=0, tiled=True)]
    unnamed x3, waiting for transfers between devices: 271 us -> 325 us
    all_to_all x1, waiting for transfers between devices: 0.01 us -> 15.9 us  [shards(): lax.all_to_all(query_heads[:, :, HR:], 'seq', split_axis=1, concat_axis=0...]
    all_to_all x1, waiting for transfers between devices: 12.5 us -> 0.01 us  [shards(): lax.all_to_all(col_out, 'seq', split_axis=0, concat_axis=1, tiled=True)]
    unnamed x69 -> x71, local copies, waits for them, and re-layouts: 22.3 us -> 23.9 us
  transfers between devices with their start and end apart: 10 -> 11, of which waited for: 8 -> 9; matrix products, arithmetic and copies ran while one was open for 10% -> 15% of each run, Pallas kernels for 0% -> 0%
where the time goes in v1:
time: 960 us; the launch traced here: 949 us
  waiting for transfers between devices  686 us (71%)
  local copies, waits for them, and re-layouts  97.1 us (10%)
  starting transfers between devices  75.5 us (8%)
  matrix products  39.7 us (4%)
  other arithmetic  25.6 us (3%)
  between operations  25.2 us (3%)
    unnamed x3, waiting for transfers between devices  325 us
    all_gather x1, waiting for transfers between devices, shards(): lax.all_gather(out_proj, ('dp', 'seq'), axis=0, tiled=True)  299 us
    unnamed x71, local copies, waits for them, and re-layouts  23.9 us
  transfers between devices with their start and end apart: 11, of which 9 were waited for; matrix products, arithmetic and copies ran while one was open for 15% of the time, Pallas kernels for 0%

profile of v1, /device:TPU:1, one launch (start us, length us, event | category | flops | bytes accessed | tf_op | source)
XLA Modules:
  0.0 948.8 jit_solution(10483223710782579403)
XLA Ops:
  42.3 12.8 %all-to-all-start.1 = ((bf16[1,512,4,128]{3,2,0,1:T(4,128)(2,1)}), bf16[1,512,4,128]{3,2,0,1:T(4,128)(2,1)}, u32[]{:S(2)}, u32[]{:S(2)}) async-start(bf16[1,512,4,128]{3,2,0,1:T(4,128)(2,1)} %copy.244), calls=%async_computation.1 | async-start | bytes 1048576 | tf_op jit(solution)/shard_map/all_to_all | solution.py:148
  55.1 2.3 copy.227
  57.4 2.3 fusion.118
  61.8 12.1 %all-to-all-done.1 = bf16[1,512,4,128]{3,2,0,1:T(4,128)(2,1)} async-done(((bf16[1,512,4,128]{3,2,0,1:T(4,128)(2,1)}), bf16[1,512,4,128]{3,2,0,1:T(4,128)(2,1)}, u32[]{:S(2)}, u32[]{:S(2)}) %all-to-all-start.1) | async-done | bytes 524320 | tf_op jit(solution)/shard_map/all_to_all | solution.py:148
  73.9 4.8 all-to-all-start.2
  80.9 15.9 %all-to-all-done.2 = bf16[1,512,4,128]{3,2,0,1:T(4,128)(2,1)} async-done(((bf16[1,512,4,128]{3,2,0,1:T(4,128)(2,1)}), bf16[1,512,4,128]{3,2,0,1:T(4,128)(2,1)}, u32[]{:S(2)}, u32[]{:S(2)}) %all-to-all-start.2) | async-done | bytes 524320 | tf_op jit(solution)/shard_map/all_to_all | solution.py:147
  96.8 5.2 all-to-all-start
  117.8 2.4 all-to-all-done
  122.1 2.8 fusion.122
  127.7 8.2 all-to-all-start.3
  135.9 2.4 fusion.27
  138.4 299.4 %all-gather.3.cloned.1.call-done = bf16[256,4,2048]{2,1,0:T(4,128)(2,1)} async-done(((bf16[1,4,2048]{2,1,0:T(4,128)(2,1)}), bf16[256,4,2048]{2,1,0:T(4,128)(2,1)}) %all-gather.3.cloned.1.call-update) | async-done | bytes 4194320 | tf_op jit(solution)/shard_map/all_gather | solution.py:136
  437.8 6.9 reshape.203
  444.7 4.5 fusion.16
  451.7 13.5 %all-to-all-start.5 = ((bf16[1,512,4,128]{3,2,0,1:T(4,128)(2,1)}), bf16[1,512,4,128]{3,2,0,1:T(4,128)(2,1)}, u32[]{:S(2)}, u32[]{:S(2)}) async-start(bf16[1,512,4,128]{3,2,0,1:T(4,128)(2,1)} %slice.155), calls=%async_computation.5 | async-start | bytes 1048576 | tf_op jit(solution)/shard_map/all_to_all | solution.py:159
  474.7 8.5 all-to-all-done.5
  483.2 4.2 stack.48
  487.3 9.9 %all-to-all-start.4 = ((bf16[256,4,2048]{2,1,0:T(4,128)(2,1)}), bf16[256,4,2048]{2,1,0:T(4,128)(2,1)}, u32[]{:S(2)}, u32[]{:S(2)}) async-start(bf16[256,4,2048]{2,1,0:T(4,128)(2,1)} %stack.48), calls=%async_computation.4 | async-start | bytes 8388608 | tf_op jit(solution)/shard_map/all_to_all | solution.py:177
  497.4 6.8 fusion.3
  507.0 324.0 %all-reduce.3.cloned.1.call-done = f32[1024,2048]{1,0:T(8,128)} async-done(((f32[1024,2048]{1,0:T(8,128)}), f32[1024,2048]{1,0:T(8,128)}) %all-reduce.3.cloned.1.call-update) | async-done | bytes 8388624
  837.1 2.5 copy.282
  839.7 3.3 fusion.113
  843.0 2.5 copy.283
  845.5 2.5 fusion.32
  861.0 10.7 %all-to-all-start.8 = ((bf16[32,16,4,128]{3,2,1,0:T(4,128)(2,1)}), bf16[32,16,4,128]{3,2,1,0:T(4,128)(2,1)}, u32[]{:S(2)}, u32[]{:S(2)}) async-start(bf16[32,16,4,128]{3,2,1,0:T(4,128)(2,1)} %copy.286), calls=%async_computation.8 | async-start | bytes 1048576 | tf_op jit(solution)/shard_map/all_to_all | solution.py:168
  873.5 7.0 reshape.189
  884.9 4.7 all-to-all-done.8
  889.6 5.5 all-to-all-start.7
  895.2 6.3 fusion.2
  904.5 8.4 all-to-all-done.7
  912.9 4.7 all-to-all-start.6
  926.1 9.6 %all-to-all-done.6 = bf16[32,16,4,128]{3,2,1,0:T(4,128)(2,1)} async-done(((bf16[32,16,4,128]{3,2,1,0:T(4,128)(2,1)}), bf16[32,16,4,128]{3,2,1,0:T(4,128)(2,1)}, u32[]{:S(2)}, u32[]{:S(2)}) %all-to-all-start.6) | async-done | bytes 524320 | tf_op jit(solution)/shard_map/all_to_all | solution.py:166
  (159 shorter events, 107.1 us)
Async XLA Ops:
  7.2 437.5 %copy-start = (bf16[1,1,512,2048]{3,2,1,0:T(8,128)(2,1)S(1)}, bf16[1,1,512,2048]{3,2,1,0:T(8,128)(2,1)}, u32[]{:S(2)}) copy-start(bf16[1,1,512,2048]{3,2,1,0:T(8,128)(2,1)} %param.13) | copy-start | bytes 6291460
  7.2 430.6 %all-gather.3.cloned.1.call-start = ((), (), s32[]{:S(2)}) async-start(), calls=%async_computation.9 | async-start | bytes 4210688 | tf_op jit(solution)/shard_map/all_gather | solution.py:136
  42.3 31.6 %all-to-all-start.1 = ((bf16[1,512,4,128]{3,2,0,1:T(4,128)(2,1)}), bf16[1,512,4,128]{3,2,0,1:T(4,128)(2,1)}, u32[]{:S(2)}, u32[]{:S(2)}) async-start(bf16[1,512,4,128]{3,2,0,1:T(4,128)(2,1)} %copy.244), calls=%async_computation.1 | async-start | bytes 1048576 | tf_op jit(solution)/shard_map/all_to_all | solution.py:148
  57.4 21.3 %copy-start.25 = (bf16[1,512,1,128]{3,1,2,0:T(8,128)(2,1)S(1)}, bf16[1,512,1,128]{3,1,2,0:T(8,128)(2,1)}, u32[]{:S(2)}) copy-start(bf16[1,512,1,128]{3,1,2,0:T(8,128)(2,1)} %get-tuple-element.54) | copy-start | bytes 393220
  57.4 21.3 %copy-start.26 = (bf16[1,512,1,128]{3,1,2,0:T(8,128)(2,1)S(1)}, bf16[1,512,1,128]{3,1,2,0:T(8,128)(2,1)}, u32[]{:S(2)}) copy-start(bf16[1,512,1,128]{3,1,2,0:T(8,128)(2,1)} %get-tuple-element.56) | copy-start | bytes 393220
  57.4 21.3 %copy-start.27 = (bf16[1,512,1,128]{3,1,2,0:T(8,128)(2,1)S(1)}, bf16[1,512,1,128]{3,1,2,0:T(8,128)(2,1)}, u32[]{:S(2)}) copy-start(bf16[1,512,1,128]{3,1,2,0:T(8,128)(2,1)} %get-tuple-element.58) | copy-start | bytes 393220
  73.9 22.9 %all-to-all-start.2 = ((bf16[1,512,4,128]{3,2,0,1:T(4,128)(2,1)}), bf16[1,512,4,128]{3,2,0,1:T(4,128)(2,1)}, u32[]{:S(2)}, u32[]{:S(2)}) async-start(bf16[1,512,4,128]{3,2,0,1:T(4,128)(2,1)} %copy.246), calls=%async_computation.2 | async-start | bytes 1048576 | tf_op jit(solution)/shard_map/all_to_all | solution.py:147
  96.8 23.4 %all-to-all-start = ((bf16[1,512,4,128]{3,2,0,1:T(4,128)(2,1)}), bf16[1,512,4,128]{3,2,0,1:T(4,128)(2,1)}, u32[]{:S(2)}, u32[]{:S(2)}) async-start(bf16[1,512,4,128]{3,2,0,1:T(4,128)(2,1)} %copy.238), calls=%async_computation | async-start | bytes 1048576 | tf_op jit(solution)/shard_map/all_to_all | solution.py:149
  104.7 2.6 copy-start.17
  106.1 4.8 copy-start.29
  109.7 1.8 copy-start.18
  109.7 2.5 copy-start.7
  127.7 324.0 %all-to-all-start.3 = ((bf16[32,16,4,128]{3,2,1,0:T(4,128)(2,1)}), bf16[32,16,4,128]{3,2,1,0:T(4,128)(2,1)}, u32[]{:S(2)}, u32[]{:S(2)}) async-start(bf16[32,16,4,128]{3,2,1,0:T(4,128)(2,1)} %copy.252), calls=%async_computation.3 | async-start | bytes 1048576 | tf_op jit(solution)/shard_map/all_to_all | solution.py:158
  451.7 31.5 %all-to-all-start.5 = ((bf16[1,512,4,128]{3,2,0,1:T(4,128)(2,1)}), bf16[1,512,4,128]{3,2,0,1:T(4,128)(2,1)}, u32[]{:S(2)}, u32[]{:S(2)}) async-start(bf16[1,512,4,128]{3,2,0,1:T(4,128)(2,1)} %slice.155), calls=%async_computation.5 | async-start | bytes 1048576 | tf_op jit(solution)/shard_map/all_to_all | solution.py:159
  465.1 2.0 copy-start.2
  471.3 11.8 %copy-start.28 = (bf16[4,2048]{1,0:T(4,128)(2,1)S(1)}, bf16[4,2048]{1,0:T(4,128)(2,1)}, u32[]{:S(2)}) copy-start(bf16[4,2048]{1,0:T(4,128)(2,1)} %param.12) | copy-start | bytes 49156
  487.3 373.7 %all-to-all-start.4 = ((bf16[256,4,2048]{2,1,0:T(4,128)(2,1)}), bf16[256,4,2048]{2,1,0:T(4,128)(2,1)}, u32[]{:S(2)}, u32[]{:S(2)}) async-start(bf16[256,4,2048]{2,1,0:T(4,128)(2,1)} %stack.48), calls=%async_computation.4 | async-start | bytes 8388608 | tf_op jit(solution)/shard_map/all_to_all | solution.py:177
  497.2 333.8 %all-reduce.3.cloned.1.call-start = ((), (), s32[]{:S(2)}) async-start(), calls=%async_computation.10 | async-start | bytes 16777216
  504.3 329.7 %copy-start.4 = (f32[4,4,128,256]{2,3,1,0:T(8,128)S(1)}, f32[4,4,128,256]{2,3,1,0:T(8,128)}, u32[]{:S(2)}) copy-start(f32[4,4,128,256]{2,3,1,0:T(8,128)} %copy-done.3) | copy-start | bytes 6291460
  850.0 2.1 copy-start.5
  856.7 2.9 copy-start.20
  859.9 11.8 %copy-start.15 = (bf16[1,4,128,4,128]{4,2,1,3,0:T(8,128)(2,1)S(1)}, bf16[1,4,128,4,128]{4,2,1,3,0:T(8,128)(2,1)}, u32[]{:S(2)}) copy-start(bf16[1,4,128,4,128]{4,2,1,3,0:T(8,128)(2,1)} %copy.284) | copy-start | bytes 1572868
  859.9 11.9 %copy-start.13 = (bf16[1,4,128,4,128]{4,2,3,1,0:T(8,128)(2,1)S(1)}, bf16[1,4,128,4,128]{4,2,3,1,0:T(8,128)(2,1)}, u32[]{:S(2)}) copy-start(bf16[1,4,128,4,128]{4,2,3,1,0:T(8,128)(2,1)} %fusion.33) | copy-start | bytes 1572868
  859.9 12.7 %copy-start.12 = (bf16[1,4,128,4,128]{4,2,3,1,0:T(8,128)(2,1)S(1)}, bf16[1,4,128,4,128]{4,2,3,1,0:T(8,128)(2,1)}, u32[]{:S(2)}) copy-start(bf16[1,4,128,4,128]{4,2,3,1,0:T(8,128)(2,1)} %fusion.29) | copy-start | bytes 1572868
  861.0 28.6 %all-to-all-start.8 = ((bf16[32,16,4,128]{3,2,1,0:T(4,128)(2,1)}), bf16[32,16,4,128]{3,2,1,0:T(4,128)(2,1)}, u32[]{:S(2)}, u32[]{:S(2)}) async-start(bf16[32,16,4,128]{3,2,1,0:T(4,128)(2,1)} %copy.286), calls=%async_computation.8 | async-start | bytes 1048576 | tf_op jit(solution)/shard_map/all_to_all | solution.py:168
  873.5 7.0 copy-start.16
  873.5 7.0 copy-start.22
  880.5 2.0 copy-start.21
  889.6 23.3 %all-to-all-start.7 = ((bf16[32,16,4,128]{3,2,1,0:T(4,128)(2,1)}), bf16[32,16,4,128]{3,2,1,0:T(4,128)(2,1)}, u32[]{:S(2)}, u32[]{:S(2)}) async-start(bf16[32,16,4,128]{3,2,1,0:T(4,128)(2,1)} %copy.277), calls=%async_computation.7 | async-start | bytes 1048576 | tf_op jit(solution)/shard_map/all_to_all | solution.py:167
  895.1 6.3 copy-start.10
  912.9 22.8 %all-to-all-start.6 = ((bf16[32,16,4,128]{3,2,1,0:T(4,128)(2,1)}), bf16[32,16,4,128]{3,2,1,0:T(4,128)(2,1)}, u32[]{:S(2)}, u32[]{:S(2)}) async-start(bf16[32,16,4,128]{3,2,1,0:T(4,128)(2,1)} %copy.269), calls=%async_computation.6 | async-start | bytes 1048576 | tf_op jit(solution)/shard_map/all_to_all | solution.py:166
  936.9 4.9 copy-start.1
  (9 other events, 10.2 us)
Sparse Core Ops, SparseCore 0:
  9.9 427.8 all-gather.2
  504.4 326.5 all-reduce.2
